TPU v7x, 256 devices: a whole 4x4x8 slice. The times are simulated.
256 devices in a mesh: nodes: 8 (over x, core), batch: 32 (over z, y).
Axes of the slice: x: 4, y: 4, z: 8, core: 2. Of those that a mesh axis runs over, the one named last changes fastest.
Arguments:
- leaves: float32 [16, 128, 4096], P('nodes', None, 'batch'), may hold values from -340 to 8
- prod_child: int32 [16, 2], replicated, may hold values from 0 to 15
- block_weight: float32 [1024, 128, 128], P('nodes'), may hold values from 0.0001 to 0.01
- block_child: int32 [8, 128], P('nodes'), may hold values from 0 to 15
- block_parent: int32 [8, 128], P('nodes'), may hold values from 0 to 3, as said below
- block_count: int32 [8], P('nodes'), may hold values from 32 to 128, as said below
- upper_flow: float32 [32, 128, 4096], P('nodes', None, 'batch'), may hold values from 0.1 to 1
Outputs:
- sum_values: float32 [32, 128, 4096], P('nodes', None, 'batch')
- leaf_flow: float32 [16, 128, 4096], P('nodes', None, 'batch')
- param_flow: float32 [1024, 128, 128], P(('nodes', 'batch'))
Inputs may be any that keep to these rules, and one draw needn't show every extreme that they name: `block_parent`: every owner's first 4 slots name its sum groups 0 to 3 in order. `block_count`: some owner has all 128 slots live.
All inputs are finite; a program needn't handle non-finite values.
Results may differ from a plain program's by a relative error of at most 0.0003.
Values sent between devices are 32-bit elements; how exact they have to be, the bound alone decides.
No kernel may reach another device: no remote copies, remote signals or barrier semaphores. Data moves between devices by JAX's collectives and lax.ppermute only.
A program may use at most 128 MiB of HBM per device.

v0:
```python
import jax
import jax.numpy as jnp
from jax import lax
from jax.sharding import PartitionSpec as P

very_low = -1e30
high = lax.Precision.HIGHEST


def body(leaves, prod_child, block_weight, block_child, block_parent, block_count, upper_flow):
    group_leaf = leaves.shape[0]
    owners = lax.axis_size("nodes")
    total_leaf = group_leaf * owners
    total_prod = prod_child.shape[0]
    prod_each = total_prod // owners
    sum_each = upper_flow.shape[0]
    blocks = block_weight.shape[0]
    mine = lax.axis_index("nodes")
    first = jax.nn.one_hot(prod_child[:, 0], total_leaf, dtype=jnp.float32)
    second = jax.nn.one_hot(prod_child[:, 1], total_leaf, dtype=jnp.float32)
    select = first + second
    own_select = lax.dynamic_slice_in_dim(select, mine * prod_each, prod_each, 0)
    columns = own_select
    own_prod = jnp.einsum(
        "pg,gjs->pjs",
        columns,
        lax.all_gather(leaves, "nodes", axis=0, tiled=True),
        precision=high,
        preferred_element_type=jnp.float32,
    )
    products = lax.all_gather(own_prod, "nodes", axis=0, tiled=True)
    peak = jnp.max(products, axis=1)
    child = block_child.reshape(-1)
    parent = block_parent.reshape(-1)
    live = jnp.arange(blocks, dtype=jnp.int32) < block_count[0]
    parent_hot = jax.nn.one_hot(parent, sum_each, dtype=jnp.float32) * live[:, None].astype(
        jnp.float32
    )
    child_peak = jnp.where(live[:, None], peak[child], very_low)
    top = jnp.max(jnp.where(parent_hot[:, :, None] > 0.0, child_peak[:, None, :], very_low), axis=0)
    diff = products[child] - top[parent][:, None, :]
    shifted = jnp.exp(jnp.where(live[:, None, None], diff, very_low))
    mixed = jnp.einsum(
        "bij,bjs->bis", block_weight, shifted, precision=high, preferred_element_type=jnp.float32
    )
    total = jnp.einsum(
        "bq,bis->qis", parent_hot, mixed, precision=high, preferred_element_type=jnp.float32
    )
    sum_values = top[:, None, :] + jnp.log(total)
    factor = upper_flow / total
    parent_factor = factor[parent]
    back = jnp.einsum(
        "bij,bis->bjs",
        block_weight,
        parent_factor,
        precision=high,
        preferred_element_type=jnp.float32,
    )
    child_term = shifted * back
    child_hot = jax.nn.one_hot(child, total_prod, dtype=jnp.float32) * live[:, None].astype(
        jnp.float32
    )
    columns = child_hot
    product_flow = lax.psum_scatter(
        jnp.einsum(
            "bc,bjs->cjs", columns, child_term, precision=high, preferred_element_type=jnp.float32
        ),
        "nodes",
        scatter_dimension=0,
        tiled=True,
    )
    columns = own_select
    leaf_flow = lax.psum_scatter(
        jnp.einsum(
            "pg,pjs->gjs", columns, product_flow, precision=high, preferred_element_type=jnp.float32
        ),
        "nodes",
        scatter_dimension=0,
        tiled=True,
    )
    param_flow = lax.psum_scatter(
        block_weight
        * jnp.einsum(
            "bis,bjs->bij",
            parent_factor,
            shifted,
            precision=high,
            preferred_element_type=jnp.float32,
        ),
        "batch",
        scatter_dimension=0,
        tiled=True,
    )
    return (sum_values, leaf_flow, param_flow)


def solution(mesh):
    placed = (
        P("nodes", None, "batch"),
        P(),
        P("nodes", None, None),
        P("nodes", None),
        P("nodes", None),
        P("nodes"),
        P("nodes", None, "batch"),
    )
    return jax.shard_map(
        body,
        mesh=mesh,
        in_specs=placed,
        out_specs=(
            P("nodes", None, "batch"),
            P("nodes", None, "batch"),
            P(("nodes", "batch"), None, None),
        ),
        check_vma=False,
    )
```

profile of v0, /device:TPU:2, one launch (start us, length us, event | category | flops | bytes accessed | tf_op | source)
XLA Modules:
  0.0 481.1 jit_solution(5586205592342857914)
XLA Ops:
  7.2 0.7 all-gather.3.cloned.1.call-update
  7.9 0.8 slice_bitcast_fusion.1
  8.9 28.1 %all-gather.3.cloned.1.call-done = f32[16,128,128]{2,1,0:T(8,128)} async-done(((f32[2,128,128]{2,1,0:T(8,128)}), f32[16,128,128]{2,1,0:T(8,128)}) %all-gather.3.cloned.1.call-update) | async-done | bytes 1048592 | tf_op jit(solution)/shard_map/all_gather | solution.py:27
  37.0 2.4 fusion.10
  39.4 0.7 copy.52
  42.8 23.1 %all-gather.5.cloned.1.call-done = f32[16,128,128]{2,1,0:T(8,128)} async-done(((f32[2,128,128]{2,1,0:T(8,128)}), f32[16,128,128]{2,1,0:T(8,128)}) %all-gather.5.cloned.1.call-update) | async-done | bytes 1048592 | tf_op jit(solution)/shard_map/all_gather | solution.py:31
  65.9 1.3 reduce_max.18
  67.8 5.5 %gather_fusion.1 = f32[128,128,128]{2,1,0:T(8,128)} fusion(f32[16,128,128]{2,1,0:T(8,128)} %all-gather.5.cloned.1.call-done, s32[1024]{0:T(1024)S(1)} %pad_clamp_fusion.1), kind=kCustom, calls=%fused_computation.1 | custom fusion | bytes 16777728 | tf_op jit(solution)/shard_map/gather | solution.py:41
  73.4 9.0 %copy.53 = f32[128,128,128]{1,2,0:T(8,128)} copy(f32[128,128,128]{2,1,0:T(8,128)} %gather_fusion.1) | data formatting | bytes 16777216 | tf_op jit(solution)/shard_map/gather | solution.py:41
  83.3 23.7 %fusion.8 = f32[128,128,128]{1,2,0:T(8,128)} fusion(f32[128,128,128]{2,1,0:T(8,128)} %param.9, f32[128,128,128]{1,2,0:T(8,128)} %copy.53, f32[128,128]{1,0:T(8,128)S(1)} %gather_fusion.2, pred[128]{0:T(512)(128)(4,1)S(1)} %get-tuple-element.22), kind=kOutput, calls=%fused_computation.14 | convolution fusion | flops 3225419776 | bytes 25231488 | tf_op jit(solution)/shard_map/bij,bjs->bis/dot_general | solution.py:43
  107.0 9.3 %copy.54 = f32[128,128,128]{2,0,1:T(8,128)} copy(f32[128,128,128]{1,2,0:T(8,128)} %fusion.8) | data formatting | bytes 16777216 | tf_op jit(solution)/shard_map/bij,bjs->bis/dot_general | solution.py:43
  116.3 6.4 %log_add_fusion = (f32[4,128,128]{2,0,1:T(4,128)S(1)}, f32[4,128,128]{2,0,1:T(4,128)S(1)}) fusion(f32[4,128]{1,0:T(4,128)S(1)} %select_reduce_fusion, f32[128,128,128]{2,0,1:T(8,128)} %copy.54, f32[128]{0:T(128)S(1)} %get-tuple-element.23, s32[128]{0:T(128)S(1)} %bitcast.40), kind=kOutput, calls=%fused_computation.19 | convolution fusion | flops 100729856 | bytes 8915968 | tf_op jit(solution)/shard_map/bq,bis->qis/dot_general | solution.py:46
  122.8 4.3 gather_fusion.3
  127.1 22.4 %bitcast_multiply_fusion = f32[128,128,128]{1,2,0:T(8,128)} fusion(f32[128,128,128]{1,2,0:T(8,128)} %copy.53, f32[128,128]{1,0:T(8,128)S(1)} %gather_fusion.2, pred[128]{0:T(512)(128)(4,1)S(1)} %get-tuple-element.22, f32[128,128,128]{2,1,0:T(8,128)} %gather_fusion.3, f32[128,128,128]{2,1,0:T(8,128)} %param.9), kind=kOutput, calls=%fused_computation.4 | convolution fusion | flops 3227516928 | bytes 33620096 | tf_op jit(solution)/shard_map/bij,bis->bjs/dot_general | solution.py:52
  149.5 9.3 %copy.57 = f32[128,128,128]{2,0,1:T(8,128)} copy(f32[128,128,128]{1,2,0:T(8,128)} %bitcast_multiply_fusion) | data formatting | bytes 16777216 | tf_op jit(solution)/shard_map/mul | solution.py:59
  158.7 6.4 %fusion.14 = f32[16,128,128]{2,0,1:T(8,128)S(1)} fusion(f32[128,128,128]{2,0,1:T(8,128)} %copy.57, f32[128]{0:T(128)S(1)} %get-tuple-element.23, s32[128]{0:T(128)S(1)} %bitcast.38), kind=kOutput, calls=%fused_computation.24 | convolution fusion | flops 402657280 | bytes 9438208 | tf_op jit(solution)/shard_map/bc,bjs->cjs/dot_general | solution.py:65
  165.1 1.3 copy.58
  166.7 33.1 %reduce-scatter.4.cloned.1.call-done = f32[2,128,128]{2,1,0:T(8,128)} async-done(((f32[16,128,128]{2,1,0:T(8,128)}), f32[2,128,128]{2,1,0:T(8,128)}) %reduce-scatter.4.cloned.1.call-update) | async-done | bytes 131088 | tf_op jit(solution)/shard_map/reduce_scatter | solution.py:64
  199.8 2.0 fusion.12
  201.9 1.4 copy.60
  203.3 16.9 %fusion.9 = f32[128,128,128]{2,1,0:T(8,128)} fusion(f32[128,128,128]{2,1,0:T(8,128)} %param.9, f32[128,128,128]{2,1,0:T(8,128)} %gather_fusion.3, f32[128,128,128]{1,2,0:T(8,128)} %copy.53, f32[128,128]{1,0:T(8,128)S(1)} %gather_fusion.2, pred[128]{0:T(512)(128)(4,1)S(1)} %get-tuple-element.22), kind=kOutput, calls=%fused_computation.15 | convolution fusion | flops 3227516928 | bytes 33620096 | tf_op jit(solution)/shard_map/bis,bjs->bij/dot_general | solution.py:83
  220.3 0.7 copy.62
  221.0 16.1 %reduce-scatter.6.cloned.1.call-done = f32[2,128,128]{2,1,0:T(8,128)} async-done(((f32[16,128,128]{2,1,0:T(8,128)}), f32[2,128,128]{2,1,0:T(8,128)}) %reduce-scatter.6.cloned.1.call-update) | async-done | bytes 131088 | tf_op jit(solution)/shard_map/reduce_scatter | solution.py:73
  237.1 237.5 %reduce-scatter.8.cloned.1.call-done = f32[4,128,128]{2,1,0:T(8,128)} async-done(((f32[128,128,128]{2,1,0:T(8,128)}), f32[4,128,128]{2,1,0:T(8,128)}) %reduce-scatter.8.cloned.1.call-update) | async-done | bytes 262160 | tf_op jit(solution)/shard_map/reduce_scatter | solution.py:81
  (28 shorter events, 4.2 us)
Async XLA Ops:
  7.2 29.8 %all-gather.3.cloned.1.call-start = ((), (), s32[]{:S(2)}) async-start(), calls=%async_computation.3 | async-start | bytes 1179648 | tf_op jit(solution)/shard_map/all_gather | solution.py:27
  7.9 58.0 %all-gather.5.cloned.1.call-start = ((), (), s32[]{:S(2)}) async-start(), calls=%async_computation.4 | async-start | bytes 1179648 | tf_op jit(solution)/shard_map/all_gather | solution.py:31
  40.1 159.7 %reduce-scatter.4.cloned.1.call-start = ((), (), s32[]{:S(2)}) async-start(), calls=%async_computation.5 | async-start | bytes 1179648 | tf_op jit(solution)/shard_map/reduce_scatter | solution.py:64
  107.0 9.3 %copy-start.2 = (s32[1,128]{1,0:T(1,128)S(1)}, s32[1,128]{1,0:T(1,128)}, u32[]{:S(2)}) copy-start(s32[1,128]{1,0:T(1,128)} %param.11) | copy-start | bytes 1540
  116.3 6.4 %copy-start = (f32[4,128,128]{2,1,0:T(8,128)S(1)}, f32[4,128,128]{2,1,0:T(8,128)}, u32[]{:S(2)}) copy-start(f32[4,128,128]{2,1,0:T(8,128)} %param.13) | copy-start | bytes 786436
  149.5 9.3 %copy-start.1 = (s32[1,128]{1,0:T(1,128)S(1)}, s32[1,128]{1,0:T(1,128)}, u32[]{:S(2)}) copy-start(s32[1,128]{1,0:T(1,128)} %param.10) | copy-start | bytes 1540
  166.5 70.6 %reduce-scatter.6.cloned.1.call-start = ((), (), s32[]{:S(2)}) async-start(), calls=%async_computation.6 | async-start | bytes 1179648 | tf_op jit(solution)/shard_map/reduce_scatter | solution.py:73
  203.3 271.3 %reduce-scatter.8.cloned.1.call-start = ((), (), s32[]{:S(2)}) async-start(), calls=%async_computation.7 | async-start | bytes 8650752 | tf_op jit(solution)/shard_map/reduce_scatter | solution.py:81
Sparse Core Ops, SparseCore 0:
  9.8 27.1 all-gather.2
  40.2 25.6 all-gather.4
  166.6 33.1 reduce-scatter.3
  203.4 33.6 reduce-scatter.5
  241.5 232.9 reduce-scatter.7
where the time goes:
time: 482 us; the launch traced here: 481 us
  waiting for transfers between devices  339 us (70%)
  matrix products  80.3 us (17%)
  local copies, waits for them, and re-layouts  43.7 us (9%)
  between operations  14.5 us (3%)
    reduce_scatter x1, waiting for transfers between devices, body(): lax.psum_scatter(block_weight * jnp.einsum('bis,bjs->bij', parent_factor,...  237 us
    reduce_scatter x1, waiting for transfers between devices, body(): lax.psum_scatter(jnp.einsum('bc,bjs->cjs', columns, child_term, precision...  33.1 us
    all_gather x1, waiting for transfers between devices, body(): lax.all_gather(leaves, 'nodes', axis=0, tiled=True)  28.1 us
    dot_general x1, matrix products, body(): jnp.einsum('bij,bjs->bis', block_weight, shifted, precision=high, preferr...  23.7 us
    all_gather x1, waiting for transfers between devices, body(): products = lax.all_gather(own_prod, 'nodes', axis=0, tiled=True)  23.1 us
    dot_general x1, matrix products, body(): jnp.einsum('bij,bis->bjs', block_weight, parent_factor, precision=high, p...  22.4 us
    dot_general x1, matrix products, body(): jnp.einsum('bis,bjs->bij', parent_factor, shifted, precision=high, prefer...  16.9 us
    reduce_scatter x1, waiting for transfers between devices, body(): lax.psum_scatter(jnp.einsum('pg,pjs->gjs', columns, product_flow, precisi...  16.1 us
  transfers between devices with their start and end apart: 5, of which 5 were waited for; matrix products, arithmetic and copies ran while one was open for 4% of the time, Pallas kernels for 0%

commit v1 on v0

--- a/solution.py
+++ b/solution.py
@@ -21,10 +21,28 @@
     select = first + second
     own_select = lax.dynamic_slice_in_dim(select, mine * prod_each, prod_each, 0)
     columns = own_select
+
+    def regions_get(vals, group_axis):
+        n_axis = lax.psum(1, group_axis)
+        frames = [(h, (h + 1) % n_axis) for h in range(n_axis)]
+        history = [(h, (h - 1) % n_axis) for h in range(n_axis)]
+        b_now, tile_out = ([vals], [vals])
+        for _ in range(n_axis // 2):
+            b_now.append(lax.ppermute(b_now[-1], group_axis, frames))
+        to_i = 0
+        while to_i < (n_axis - 1) // 2:
+            tile_out.append(lax.ppermute(tile_out[-1], group_axis, history))
+            to_i = to_i + 1
+        return jnp.roll(
+            jnp.concatenate([*b_now[::-1], *tile_out[1:]], 0),
+            (lax.axis_index(group_axis) - n_axis // 2) * vals.shape[0],
+            0,
+        )
+
     own_prod = jnp.einsum(
         "pg,gjs->pjs",
         columns,
-        lax.all_gather(leaves, "nodes", axis=0, tiled=True),
+        regions_get(leaves, "nodes"),
         precision=high,
         preferred_element_type=jnp.float32,
     )

time: 482 us -> 473 us (0.981)
  waiting for transfers between devices: 339 us -> 324 us
  starting transfers between devices: 0.42 us -> 6.05 us
    all_gather x1 -> x0, waiting for transfers between devices: 28.1 us -> none  [body(): lax.all_gather(leaves, 'nodes', axis=0, tiled=True)]
    ppermute x0 -> x7, waiting for transfers between devices: none -> 11 us  [the longest x4 10.8 us: regions_get(): b_now.append(lax.ppermute(b_now[-1], group_axis, frames))]
    ppermute x0 -> x7, starting transfers between devices: none -> 5.66 us  [the longest x3 5.64 us: regions_get(): tile_out.append(lax.ppermute(tile_out[-1], group_axis, history))]
  transfers between devices with their start and end apart: 5 -> 11, of which waited for: 5 -> 9; matrix products, arithmetic and copies ran while one was open for 4% -> 4% of each run, Pallas kernels for 0% -> 0%
where the time goes in v1:
time: 473 us
  waiting for transfers between devices  324 us (68%)
  matrix products  78.6 us (17%)
  local copies, waits for them, and re-layouts  46.8 us (10%)
  between operations  14.5 us (3%)
  starting transfers between devices  6.05 us (1%)
    reduce_scatter x1, waiting for transfers between devices, body(): lax.psum_scatter(block_weight * jnp.einsum('bis,bjs->bij', parent_factor,...  237 us
    reduce_scatter x1, waiting for transfers between devices, body(): lax.psum_scatter(jnp.einsum('bc,bjs->cjs', columns, child_term, precision...  33.1 us
    all_gather x1, waiting for transfers between devices, body(): products = lax.all_gather(own_prod, 'nodes', axis=0, tiled=True)  27 us
    dot_general x1, matrix products, body(): jnp.einsum('bij,bjs->bis', block_weight, shifted, precision=high, preferr...  23.7 us
    dot_general x1, matrix products, body(): jnp.einsum('bij,bis->bjs', block_weight, parent_factor, precision=high, p...  22.4 us
    dot_general x1, matrix products, body(): jnp.einsum('bis,bjs->bij', parent_factor, shifted, precision=high, prefer...  16.9 us
    reduce_scatter x1, waiting for transfers between devices, body(): lax.psum_scatter(jnp.einsum('pg,pjs->gjs', columns, product_flow, precisi...  16 us
    gather x3, local copies, waits for them, and re-layouts, body(): diff = products[child] - top[parent][:, None, :]  15.3 us
  transfers between devices with their start and end apart: 11, of which 9 were waited for; matrix products, arithmetic and copies ran while one was open for 4% of the time, Pallas kernels for 0%

profile of v1, /device:TPU:2, one launch (start us, length us, event | category | flops | bytes accessed | tf_op | source)
XLA Modules:
  0.0 472.7 jit_solution(2668815109971319671)
XLA Ops:
  8.2 1.7 collective-permute-start.4
  10.0 2.6 collective-permute-done
  12.6 2.0 collective-permute-start.5
  14.7 2.4 collective-permute-done.1
  17.2 1.9 collective-permute-start.6
  19.1 2.4 collective-permute-done.2
  22.3 3.5 collective-permute-done.3
  25.8 1.9 concatenate.6
  31.8 27.0 %all-gather.2.cloned.1.call-done = f32[16,128,128]{2,1,0:T(8,128)} async-done(((f32[2,128,128]{2,1,0:T(8,128)}), f32[16,128,128]{2,1,0:T(8,128)}) %all-gather.2.cloned.1.call-update) | async-done | bytes 1048592 | tf_op jit(solution)/shard_map/all_gather | solution.py:49
  58.8 5.5 %gather_fusion.1 = f32[128,128,128]{2,1,0:T(8,128)} fusion(f32[16,128,128]{2,1,0:T(8,128)} %all-gather.2.cloned.1.call-done, s32[1024]{0:T(1024)S(1)} %pad_clamp_fusion.1), kind=kCustom, calls=%fused_computation.1 | custom fusion | bytes 16777728 | tf_op jit(solution)/shard_map/gather | solution.py:59
  64.3 9.1 %copy.68 = f32[128,128,128]{1,2,0:T(8,128)} copy(f32[128,128,128]{2,1,0:T(8,128)} %gather_fusion.1) | data formatting | bytes 16777216 | tf_op jit(solution)/shard_map/gather | solution.py:59
  75.0 23.7 %fusion.8 = f32[128,128,128]{1,2,0:T(8,128)} fusion(f32[128,128,128]{2,1,0:T(8,128)} %param.9, f32[128,128,128]{1,2,0:T(8,128)} %copy.68, f32[128,128]{1,0:T(8,128)S(1)} %gather_fusion.2, pred[128]{0:T(512)(128)(4,1)S(1)} %get-tuple-element.22), kind=kOutput, calls=%fused_computation.14 | convolution fusion | flops 3225419776 | bytes 25231488 | tf_op jit(solution)/shard_map/bij,bjs->bis/dot_general | solution.py:61
  98.8 9.3 %copy.69 = f32[128,128,128]{2,0,1:T(8,128)} copy(f32[128,128,128]{1,2,0:T(8,128)} %fusion.8) | data formatting | bytes 16777216 | tf_op jit(solution)/shard_map/bij,bjs->bis/dot_general | solution.py:61
  108.0 6.4 %log_add_fusion = (f32[4,128,128]{2,0,1:T(4,128)S(1)}, f32[4,128,128]{2,0,1:T(4,128)S(1)}) fusion(f32[4,128]{1,0:T(4,128)S(1)} %select_reduce_fusion, f32[128,128,128]{2,0,1:T(8,128)} %copy.69, f32[128]{0:T(128)S(1)} %get-tuple-element.23, s32[128]{0:T(128)S(1)} %bitcast.40), kind=kOutput, calls=%fused_computation.19 | convolution fusion | flops 100729856 | bytes 8915968 | tf_op jit(solution)/shard_map/bq,bis->qis/dot_general | solution.py:64
  114.5 4.3 gather_fusion.3
  118.9 22.4 %bitcast_multiply_fusion = f32[128,128,128]{1,2,0:T(8,128)} fusion(f32[128,128,128]{1,2,0:T(8,128)} %copy.68, f32[128,128]{1,0:T(8,128)S(1)} %gather_fusion.2, pred[128]{0:T(512)(128)(4,1)S(1)} %get-tuple-element.22, f32[128,128,128]{2,1,0:T(8,128)} %gather_fusion.3, f32[128,128,128]{2,1,0:T(8,128)} %param.9), kind=kOutput, calls=%fused_computation.4 | convolution fusion | flops 3227516928 | bytes 33620096 | tf_op jit(solution)/shard_map/bij,bis->bjs/dot_general | solution.py:70
  141.2 9.3 %copy.72 = f32[128,128,128]{2,0,1:T(8,128)} copy(f32[128,128,128]{1,2,0:T(8,128)} %bitcast_multiply_fusion) | data formatting | bytes 16777216 | tf_op jit(solution)/shard_map/mul | solution.py:77
  150.6 6.4 %fusion.14 = f32[16,128,128]{2,0,1:T(8,128)S(1)} fusion(f32[128,128,128]{2,0,1:T(8,128)} %copy.72, f32[128]{0:T(128)S(1)} %get-tuple-element.23, s32[128]{0:T(128)S(1)} %bitcast.38), kind=kOutput, calls=%fused_computation.24 | convolution fusion | flops 402657280 | bytes 9438208 | tf_op jit(solution)/shard_map/bc,bjs->cjs/dot_general | solution.py:83
  158.5 33.1 %reduce-scatter.4.cloned.1.call-done = f32[2,128,128]{2,1,0:T(8,128)} async-done(((f32[16,128,128]{2,1,0:T(8,128)}), f32[2,128,128]{2,1,0:T(8,128)}) %reduce-scatter.4.cloned.1.call-update) | async-done | bytes 131088 | tf_op jit(solution)/shard_map/reduce_scatter | solution.py:82
  191.6 2.0 fusion.12
  193.7 1.4 copy.75
  195.1 16.9 %fusion.9 = f32[128,128,128]{2,1,0:T(8,128)} fusion(f32[128,128,128]{2,1,0:T(8,128)} %param.9, f32[128,128,128]{2,1,0:T(8,128)} %gather_fusion.3, f32[128,128,128]{1,2,0:T(8,128)} %copy.68, f32[128,128]{1,0:T(8,128)S(1)} %gather_fusion.2, pred[128]{0:T(512)(128)(4,1)S(1)} %get-tuple-element.22), kind=kOutput, calls=%fused_computation.15 | convolution fusion | flops 3227516928 | bytes 33620096 | tf_op jit(solution)/shard_map/bis,bjs->bij/dot_general | solution.py:101
  212.8 16.0 %reduce-scatter.6.cloned.1.call-done = f32[2,128,128]{2,1,0:T(8,128)} async-done(((f32[16,128,128]{2,1,0:T(8,128)}), f32[2,128,128]{2,1,0:T(8,128)}) %reduce-scatter.6.cloned.1.call-update) | async-done | bytes 131088 | tf_op jit(solution)/shard_map/reduce_scatter | solution.py:91
  228.8 237.4 %reduce-scatter.8.cloned.1.call-done = f32[4,128,128]{2,1,0:T(8,128)} async-done(((f32[128,128,128]{2,1,0:T(8,128)}), f32[4,128,128]{2,1,0:T(8,128)}) %reduce-scatter.8.cloned.1.call-update) | async-done | bytes 262160 | tf_op jit(solution)/shard_map/reduce_scatter | solution.py:99
  (43 shorter events, 9.6 us)
Async XLA Ops:
  7.2 51.6 %all-gather.2.cloned.1.call-start = ((), (), s32[]{:S(2)}) async-start(), calls=%async_computation.3 | async-start | bytes 1179648 | tf_op jit(solution)/shard_map/all_gather | solution.py:49
  8.2 4.4 collective-permute-start
  8.2 4.4 collective-permute-start.4
  12.6 4.4 collective-permute-start.1
  12.6 4.6 collective-permute-start.5
  17.0 4.4 collective-permute-start.2
  17.2 5.1 %collective-permute-start.6 = (f32[2,128,128]{2,0,1:T(2,128)S(1)}, f32[2,128,128]{2,0,1:T(2,128)S(1)}, u32[]{:S(2)}, u32[]{:S(2)}) collective-permute-start(f32[2,128,128]{2,0,1:T(2,128)S(1)} %collective-permute-done.5), channel_id=1, source_target_pairs={{0,224},{32,0},{64,32},{96,64},{128,96},{160,128},{192,160},{224,1... | collective-permute-start | bytes 393224 | tf_op jit(solution)/shard_map/ppermute | solution.py:34
  21.4 4.4 collective-permute-start.3
  29.1 162.5 %reduce-scatter.4.cloned.1.call-start = ((), (), s32[]{:S(2)}) async-start(), calls=%async_computation.4 | async-start | bytes 1179648 | tf_op jit(solution)/shard_map/reduce_scatter | solution.py:82
  64.3 9.1 %copy-start = (f32[16,128,128]{2,1,0:T(8,128)S(1)}, f32[16,128,128]{2,1,0:T(8,128)}, u32[]{:S(2)}) copy-start(f32[16,128,128]{2,1,0:T(8,128)} %all-gather.2.cloned.1.call-done) | copy-start | bytes 3145732
  98.8 9.3 %copy-start.3 = (s32[1,128]{1,0:T(1,128)S(1)}, s32[1,128]{1,0:T(1,128)}, u32[]{:S(2)}) copy-start(s32[1,128]{1,0:T(1,128)} %param.11) | copy-start | bytes 1540
  108.0 6.4 %copy-start.1 = (f32[4,128,128]{2,1,0:T(8,128)S(1)}, f32[4,128,128]{2,1,0:T(8,128)}, u32[]{:S(2)}) copy-start(f32[4,128,128]{2,1,0:T(8,128)} %param.13) | copy-start | bytes 786436
  141.2 9.3 %copy-start.2 = (s32[1,128]{1,0:T(1,128)S(1)}, s32[1,128]{1,0:T(1,128)}, u32[]{:S(2)}) copy-start(s32[1,128]{1,0:T(1,128)} %param.10) | copy-start | bytes 1540
  158.3 70.6 %reduce-scatter.6.cloned.1.call-start = ((), (), s32[]{:S(2)}) async-start(), calls=%async_computation.5 | async-start | bytes 1179648 | tf_op jit(solution)/shard_map/reduce_scatter | solution.py:91
  195.1 271.1 %reduce-scatter.8.cloned.1.call-start = ((), (), s32[]{:S(2)}) async-start(), calls=%async_computation.6 | async-start | bytes 8650752 | tf_op jit(solution)/shard_map/reduce_scatter | solution.py:99
Sparse Core Ops, SparseCore 0:
  29.2 29.5 all-gather.1
  158.4 33.1 reduce-scatter.3
  195.2 33.5 reduce-scatter.5
  233.3 232.8 reduce-scatter.7
